TPU v7x, 256 devices: a whole 4x4x8 slice. The times are simulated.
256 devices in a mesh: clus: 4 (over z_lo, core), sub: 64 (over x, z_hi, y).
Axes of the slice: x: 4, y: 4, z: 8 (z_hi: 4, z_lo: 2; z = z_hi * 2 + z_lo), core: 2. Of those that a mesh axis runs over, the one named last changes fastest.
Arguments:
- load: float32 [4, 64, 6, 256, 128], P('clus', 'sub'), may hold values from -30 to 30
- dual_op: float32 [4, 64, 1536, 1536], P('clus', 'sub'), may hold values from -6 to 17, as said below
- modes: float32 [4, 64, 32, 1536], P('clus', 'sub'), may hold values from -1 to 1
- face_map: int32 [4, 64, 3, 256], P('clus', 'sub'), may hold values from 0 to 255, each once within a row
- cluster: int32 [4, 64], P('clus', 'sub'), may hold values from 0 to 1, as said below
Outputs:
- multipliers: float32 [4, 64, 6, 256, 128], P('clus', 'sub')
- residual: float32 [4, 64, 6, 256, 128], P('clus', 'sub')
Inputs may be any that keep to these rules, and one draw needn't show every extreme that they name: `dual_op`: each subdomain's block is symmetric positive definite. `face_map`: each row of 256 entries names every row of the neighbour's face once. In every cluster group exactly half of the 64 subdomains belong to each of its two clusters.
All inputs are finite; a program needn't handle non-finite values.
Results may differ from a plain program's by a relative error of at most 0.00011.
Values sent between devices are 32-bit elements; how exact they have to be, the bound alone decides.
No kernel may reach another device: no remote copies, remote signals or barrier semaphores. Data moves between devices by JAX's collectives and lax.ppermute only.
A program may use at most 128 MiB of HBM per device.

v0:
```python
import jax
import jax.numpy as jnp
from jax import lax
from jax.sharding import PartitionSpec as P

FACE = 256
COLS = 128
ITERS = 3
ORDER = 1536
damping_factor = 0.8
highest = lax.Precision.HIGHEST


def with_halo(cells, sides, width):
    for axis, dim in sides:
        count = lax.axis_size(axis)
        head = lax.slice_in_dim(cells, 0, width, axis=dim)
        tail = lax.slice_in_dim(cells, cells.shape[dim] - width, cells.shape[dim], axis=dim)
        cells = jnp.concatenate(
            [
                lax.ppermute(tail, axis, [(i, (i + 1) % count) for i in range(count)]),
                cells,
                lax.ppermute(head, axis, [((i + 1) % count, i) for i in range(count)]),
            ],
            axis=dim,
        )
    return cells


def from_partner(array, axis, distance):
    return lax.ppermute(array, axis, [(i, i ^ 1 << distance) for i in range(lax.axis_size(axis))])


def partner_values(values, pairing, inverse):
    result = []
    for direction in range(3):
        plus_face = values[2 * direction]
        minus_face = values[2 * direction + 1]
        upward = jnp.take(plus_face, inverse[direction], axis=0)
        width = upward.shape[0]
        if direction == 0:
            arrived = with_halo(jnp.concatenate([minus_face, upward], axis=0), (("sub", 0),), width)
            from_minus = arrived[:width]
            from_plus = arrived[3 * width :]
        elif direction == 1:
            arrived = with_halo(
                jnp.concatenate([minus_face, upward], axis=0), (("clus", 0),), width
            )
            from_minus = arrived[:width]
            from_plus = arrived[3 * width :]
        else:
            bit_index = lax.axis_size("sub").bit_length() - 2
            arrived = from_partner(jnp.stack([upward, minus_face]), "sub", bit_index)
            from_minus = arrived[0]
            from_plus = arrived[1]
        plus_side = jnp.take(from_plus, pairing[direction], axis=0)
        result += [plus_side, from_minus]
    return jnp.stack(result)


def solve_one(lower_part, column_block):
    return jax.scipy.linalg.cho_solve((lower_part, True), column_block)


def per_device(load, dual_op, modes, face_map, cluster):
    values = load[0, 0]
    operator = dual_op[0, 0]
    mode_rows = modes[0, 0]
    pairing = face_map[0, 0]
    member = cluster[0, 0]
    inverse = jnp.argsort(pairing, axis=-1)
    plus_owned = pairing % 2 == 0
    minus_owned = jnp.broadcast_to(jnp.arange(FACE) % 2 == 1, plus_owned.shape)
    owned = jnp.stack([plus_owned, minus_owned], axis=1).reshape(6, FACE, 1).astype(jnp.float32)
    selector = (jnp.arange(2) == member).astype(jnp.float32)
    weighted = mode_rows * owned.reshape(1, ORDER)
    gram_terms = jnp.einsum("mn,kn->mk", weighted, mode_rows, precision=highest)
    gram_total = lax.psum(selector[:, None, None] * gram_terms[None], "sub")
    factor = jnp.linalg.cholesky(gram_total)
    residual = values * owned
    multipliers = jnp.zeros_like(values)
    for iteration in range(ITERS):
        projected = jnp.einsum(
            "mn,nc->mc", mode_rows, residual.reshape(ORDER, COLS), precision=highest
        )
        gathered = lax.psum(selector[:, None, None] * projected[None], "sub")
        coefficients = jax.vmap(solve_one)(factor, gathered)
        own_coeff = lax.dynamic_index_in_dim(coefficients, member, 0, keepdims=False)
        correction = jnp.einsum("mn,mc->nc", mode_rows, own_coeff, precision=highest).reshape(
            6, FACE, COLS
        )
        search = residual - owned * correction
        local_copy = search - (1.0 - owned) * partner_values(search, pairing, inverse)
        applied = jnp.dot(operator, local_copy.reshape(ORDER, COLS), precision=highest).reshape(
            6, FACE, COLS
        )
        assembled = owned * (applied - partner_values(applied, pairing, inverse))
        numerator, denominator = lax.psum(
            (jnp.sum(residual * search, axis=(0, 1)), jnp.sum(search * assembled, axis=(0, 1))),
            ("clus", "sub"),
        )
        step_size = damping_factor * numerator / denominator
        multipliers = multipliers + step_size * search
        residual = residual - step_size * assembled
    return (multipliers[None, None], residual[None, None])


def solution(mesh):
    placed = (
        P("clus", "sub", None, None, None),
        P("clus", "sub", None, None),
        P("clus", "sub", None, None),
        P("clus", "sub", None, None),
        P("clus", "sub"),
    )
    return jax.shard_map(
        per_device,
        mesh=mesh,
        in_specs=placed,
        out_specs=(P("clus", "sub", None, None, None), P("clus", "sub", None, None, None)),
        check_vma=False,
    )
```

profile of v0, /device:TPU:1, one launch (start us, length us, event | category | flops | bytes accessed | tf_op | source)
XLA Modules:
  0.0 1692.0 jit_solution(10219532640262902524)
XLA Ops:
  22.2 326.7 %all-reduce.3 = (f32[2,32,128]{2,1,0:T(8,128)S(1)}, f32[2,32,32]{1,2,0:T(8,128)S(1)}) all-reduce(f32[2,32,128]{2,1,0:T(8,128)S(1)} %broadcast_multiply_fusion.3, f32[2,32,32]{1,2,0:T(8,128)S(1)} %broadcast_multiply_fusion.4), channel_id=1, replica_groups=mesh['clus'=4,'sub'=64] {'sub'}, use_global_device_ids=true, to_apply=%region_3.4 | all-reduce | flops 10240 | bytes 81920 | tf_op jit(solution)/shard_map/psum | solution.py:86
  349.0 5.9 custom-call.9
  355.1 4.9 custom-call.12
  360.4 1.8 convolution_bitcast_fusion.2
  363.6 2.1 multiply_subtract_fusion.9
  366.9 1.9 slice_bitcast_fusion.19
  373.3 56.8 %collective-permute-start.3 = (f32[256,128]{0,1:T(8,128)}, f32[256,128]{0,1:T(8,128)}, u32[]{:S(2)}, u32[]{:S(2)}) collective-permute-start(f32[256,128]{0,1:T(8,128)} %broadcast_select_fusion.10), channel_id=1, source_target_pairs={{0,64},{64,128},{128,192},{192,0},{1,65},{65,129},{129,193},{193,1... | collective-permute-start | bytes 393224 | tf_op jit(solution)/shard_map/ppermute | solution.py:21
  430.1 8.1 collective-permute-start
  439.5 3.8 collective-permute-done
  454.5 12.2 fusion.6
  472.0 8.7 collective-permute-start.5
  487.9 7.4 collective-permute-done.6
  497.9 1.6 multiply_reduce_fusion.5
  500.7 77.2 %all-reduce.2 = (f32[128]{0:T(128)S(1)}, f32[128]{0:T(128)S(1)}) all-reduce(f32[128]{0:T(128)S(1)} %get-tuple-element.13, f32[128]{0:T(128)S(1)} %get-tuple-element.12), channel_id=1, replica_groups=mesh['clus'=4,'sub'=64] {'clus','sub'}, use_global_device_ids=true, to_apply=%region_8.11 | all-reduce | flops 256 | bytes 2048 | tf_op jit(solution)/shard_map/psum | solution.py:98
  581.6 316.0 %psum.74 = f32[2,32,128]{2,1,0:T(8,128)S(1)} all-reduce(f32[2,32,128]{2,1,0:T(8,128)S(1)} %broadcast_multiply_fusion.2), channel_id=1, replica_groups=mesh['clus'=4,'sub'=64] {'sub'}, use_global_device_ids=true, to_apply=%region_9.12 | all-reduce | flops 8192 | bytes 65536 | tf_op jit(solution)/shard_map/psum | solution.py:86
  900.0 2.3 copy.260
  902.3 2.6 multiply_subtract_fusion.6
  913.0 56.4 %collective-permute-start.12 = (f32[256,128]{0,1:T(8,128)}, f32[256,128]{0,1:T(8,128)S(1)}, u32[]{:S(2)}, u32[]{:S(2)}) collective-permute-start(f32[256,128]{0,1:T(8,128)} %get-tuple-element.53), channel_id=1, source_target_pairs={{64,0},{128,64},{192,128},{0,192},{65,1},{129,65},{193,129},{1,193... | collective-permute-start | bytes 393224 | tf_op jit(solution)/shard_map/ppermute | solution.py:23
  970.8 2.3 copy.292
  974.5 2.5 collective-permute-start.13
  977.0 1.6 pad_maximum_fusion.2
  982.3 2.4 collective-permute-done.11
  994.1 12.1 fusion.9
  1011.5 1.6 collective-permute-start.17
  1013.1 4.6 collective-permute-start.15
  1021.1 1.9 collective-permute-start.18
  1023.0 1.6 pad_maximum_fusion.3
  1029.9 1.9 collective-permute-done.16
  1042.0 2.3 copy.294
  1044.3 1.9 multiply_reduce_fusion.3
  1046.2 77.9 %all-reduce.1 = (f32[128]{0:T(128)S(1)}, f32[128]{0:T(128)S(1)}) all-reduce(f32[128]{0:T(128)S(1)} %get-tuple-element.17, f32[128]{0:T(128)S(1)} %get-tuple-element.16), channel_id=1, replica_groups=mesh['clus'=4,'sub'=64] {'clus','sub'}, use_global_device_ids=true, to_apply=%region_13.16 | all-reduce | flops 256 | bytes 2048 | tf_op jit(solution)/shard_map/psum | solution.py:98
  1128.3 316.1 %psum.77 = f32[2,32,128]{2,1,0:T(8,128)S(1)} all-reduce(f32[2,32,128]{2,1,0:T(8,128)S(1)} %broadcast_multiply_fusion.1), channel_id=1, replica_groups=mesh['clus'=4,'sub'=64] {'sub'}, use_global_device_ids=true, to_apply=%region_14.17 | all-reduce | flops 8192 | bytes 65536 | tf_op jit(solution)/shard_map/psum | solution.py:86
  1448.0 2.8 multiply_subtract_fusion.2
  1456.7 56.1 %collective-permute-start.22 = (f32[256,128]{0,1:T(8,128)}, f32[256,128]{0,1:T(8,128)S(1)}, u32[]{:S(2)}, u32[]{:S(2)}) collective-permute-start(f32[256,128]{0,1:T(8,128)} %get-tuple-element.41), channel_id=1, source_target_pairs={{64,0},{128,64},{192,128},{0,192},{65,1},{129,65},{193,129},{1,193... | collective-permute-start | bytes 393224 | tf_op jit(solution)/shard_map/ppermute | solution.py:23
  1514.0 2.3 copy.329
  1517.8 2.3 collective-permute-start.23
  1524.1 3.9 collective-permute-done.21
  1536.6 12.4 fusion.12
  1555.6 3.3 collective-permute-start.25
  1560.5 3.7 collective-permute-start.28
  1564.2 1.7 pad_maximum_fusion.5
  1570.3 1.8 bitcast_dynamic-update-slice_fusion.5
  1579.8 1.7 bitcast_dynamic-update-slice_fusion.3
  1587.6 1.6 bitcast_dynamic-update-slice_fusion.8
  1595.4 1.9 multiply_reduce_fusion.1
  1597.3 76.0 %all-reduce = (f32[128]{0:T(128)S(1)}, f32[128]{0:T(128)S(1)}) all-reduce(f32[128]{0:T(128)S(1)} %get-tuple-element.15, f32[128]{0:T(128)S(1)} %get-tuple-element.14), channel_id=1, replica_groups=mesh['clus'=4,'sub'=64] {'clus','sub'}, use_global_device_ids=true, to_apply=%region_18.21 | all-reduce | flops 256 | bytes 2048 | tf_op jit(solution)/shard_map/psum | solution.py:98
  1673.2 1.7 bitcast_dynamic-update-slice_fusion.1
  1678.7 3.7 multiply_subtract_fusion
  (403 shorter events, 171.5 us)
Async XLA Ops:
  12.9 473.6 %copy-start.20 = (s32[1024]{0:T(1024)}, s32[1024]{0:T(1024)S(1)}, u32[]{:S(2)}) copy-start(s32[1024]{0:T(1024)S(1)} %pad_clamp_fusion.5) | copy-start | bytes 12292
  12.9 347.4 %copy-start.41 = (f32[2]{0:T(128)}, f32[2]{0:T(128)S(1)}, u32[]{:S(2)}) copy-start(f32[2]{0:T(128)S(1)} %compare_convert_fusion) | copy-start | bytes 28
  15.7 438.8 %copy-start.1 = (f32[1536,128]{0,1:T(8,128)}, f32[1536,128]{0,1:T(8,128)S(1)}, u32[]{:S(2)}) copy-start(f32[1536,128]{0,1:T(8,128)S(1)} %copy.224) | copy-start | bytes 2359300
  18.3 451.4 %copy-start.22 = (s32[1024]{0:T(1024)}, s32[1024]{0:T(1024)S(1)}, u32[]{:S(2)}) copy-start(s32[1024]{0:T(1024)S(1)} %pad_clamp_fusion.4) | copy-start | bytes 12292
  19.2 352.7 %copy-start.23 = (pred[256]{0:T(512)(128)(4,1)S(1)}, pred[256]{0:T(512)(128)(4,1)}, u32[]{:S(2)}) copy-start(pred[256]{0:T(512)(128)(4,1)} %get-tuple-element.87) | copy-start | bytes 772
  19.2 353.4 %copy-start.26 = (pred[256]{0:T(512)(128)(4,1)S(1)}, pred[256]{0:T(512)(128)(4,1)}, u32[]{:S(2)}) copy-start(pred[256]{0:T(512)(128)(4,1)} %get-tuple-element.86) | copy-start | bytes 772
  19.3 418.9 %copy-start.29 = (pred[256]{0:T(512)(128)(4,1)S(1)}, pred[256]{0:T(512)(128)(4,1)}, u32[]{:S(2)}) copy-start(pred[256]{0:T(512)(128)(4,1)} %get-tuple-element.85) | copy-start | bytes 772
  362.2 85.2 %copy-start.35 = (pred[256]{0:T(512)(128)(4,1)S(1)}, pred[256]{0:T(512)(128)(4,1)}, u32[]{:S(2)}) copy-start(pred[256]{0:T(512)(128)(4,1)} %compare_and_fusion.3) | copy-start | bytes 772
  363.6 86.9 %copy-start.32 = (pred[256]{0:T(512)(128)(4,1)S(1)}, pred[256]{0:T(512)(128)(4,1)}, u32[]{:S(2)}) copy-start(pred[256]{0:T(512)(128)(4,1)} %compare_and_fusion) | copy-start | bytes 772
  372.6 73.2 %collective-permute-start.1 = (f32[256,128]{0,1:T(8,128)}, f32[256,128]{0,1:T(8,128)}, u32[]{:S(2)}, u32[]{:S(2)}) collective-permute-start(f32[256,128]{0,1:T(8,128)} %broadcast_select_fusion.11), channel_id=1, source_target_pairs={{0,1},{1,2},{2,3},{3,4},{4,5},{5,6},{6,7},{7,8},{8,9},{9,10},{10,1... | collective-permute-start | bytes 393224 | tf_op jit(solution)/shard_map/ppermute | solution.py:21
  373.3 74.7 %collective-permute-start.3 = (f32[256,128]{0,1:T(8,128)}, f32[256,128]{0,1:T(8,128)}, u32[]{:S(2)}, u32[]{:S(2)}) collective-permute-start(f32[256,128]{0,1:T(8,128)} %broadcast_select_fusion.10), channel_id=1, source_target_pairs={{0,64},{64,128},{128,192},{192,0},{1,65},{65,129},{129,193},{193,1... | collective-permute-start | bytes 393224 | tf_op jit(solution)/shard_map/ppermute | solution.py:21
  430.1 8.4 collective-permute-start.2
  430.1 13.2 collective-permute-start
  438.2 11.4 collective-permute-start.4
  470.5 14.9 collective-permute-start.7
  472.0 14.3 collective-permute-start.5
  482.8 97.2 %copy-start = (f32[1,1,32,1536]{3,2,1,0:T(8,128)S(1)}, f32[1,1,32,1536]{3,2,1,0:T(8,128)}, u32[]{:S(2)}) copy-start(f32[1,1,32,1536]{3,2,1,0:T(8,128)} %param.11) | copy-start | bytes 589828
  484.0 11.3 collective-permute-start.6
  484.0 12.0 collective-permute-start.8
  485.4 10.6 collective-permute-start.9
  497.0 407.9 %copy-start.8 = (f32[256,128]{0,1:T(8,128)}, f32[256,128]{0,1:T(8,128)S(1)}, u32[]{:S(2)}) copy-start(f32[256,128]{0,1:T(8,128)S(1)} %copy.251) | copy-start | bytes 393220
  902.3 87.0 %copy-start.33 = (pred[256]{0:T(512)(128)(4,1)S(1)}, pred[256]{0:T(512)(128)(4,1)}, u32[]{:S(2)}) copy-start(pred[256]{0:T(512)(128)(4,1)} %compare_and_fusion) | copy-start | bytes 772
  906.0 88.1 %copy-start.4 = (f32[1536,128]{0,1:T(8,128)S(1)}, f32[1536,128]{0,1:T(8,128)}, u32[]{:S(2)}) copy-start(f32[1536,128]{0,1:T(8,128)} %copy-done.3) | copy-start | bytes 2359300
  913.0 65.8 %collective-permute-start.12 = (f32[256,128]{0,1:T(8,128)}, f32[256,128]{0,1:T(8,128)S(1)}, u32[]{:S(2)}, u32[]{:S(2)}) collective-permute-start(f32[256,128]{0,1:T(8,128)} %get-tuple-element.53), channel_id=1, source_target_pairs={{64,0},{128,64},{192,128},{0,192},{65,1},{129,65},{193,129},{1,193... | collective-permute-start | bytes 393224 | tf_op jit(solution)/shard_map/ppermute | solution.py:23
  969.5 10.3 collective-permute-start.10
  973.0 11.6 collective-permute-start.11
  974.5 11.1 collective-permute-start.13
  978.6 8.6 collective-permute-start.14
  1011.5 13.1 collective-permute-start.17
  1013.1 13.3 collective-permute-start.15
  1021.1 10.8 collective-permute-start.16
  1021.1 12.4 collective-permute-start.18
  1024.6 9.8 collective-permute-start.19
  1039.3 411.5 %copy-start.13 = (f32[256,128]{0,1:T(8,128)}, f32[256,128]{0,1:T(8,128)S(1)}, u32[]{:S(2)}) copy-start(f32[256,128]{0,1:T(8,128)S(1)} %copy.287) | copy-start | bytes 393220
  1448.0 84.7 %copy-start.34 = (pred[256]{0:T(512)(128)(4,1)S(1)}, pred[256]{0:T(512)(128)(4,1)}, u32[]{:S(2)}) copy-start(pred[256]{0:T(512)(128)(4,1)} %compare_and_fusion) | copy-start | bytes 772
  1456.7 63.8 %collective-permute-start.22 = (f32[256,128]{0,1:T(8,128)}, f32[256,128]{0,1:T(8,128)S(1)}, u32[]{:S(2)}, u32[]{:S(2)}) collective-permute-start(f32[256,128]{0,1:T(8,128)} %get-tuple-element.41), channel_id=1, source_target_pairs={{64,0},{128,64},{192,128},{0,192},{65,1},{129,65},{193,129},{1,193... | collective-permute-start | bytes 393224 | tf_op jit(solution)/shard_map/ppermute | solution.py:23
  1512.7 8.7 collective-permute-start.20
  1516.3 11.6 collective-permute-start.21
  1517.8 12.4 collective-permute-start.23
  1520.1 11.7 collective-permute-start.24
  1555.6 117.7 %copy-start.9 = (f32[256,128]{0,1:T(8,128)S(1)}, f32[256,128]{0,1:T(8,128)}, u32[]{:S(2)}) copy-start(f32[256,128]{0,1:T(8,128)} %copy-done.8) | copy-start | bytes 393220
  1555.6 12.7 collective-permute-start.25
  1560.4 118.3 %copy-start.7 = (f32[1,1,6,256,128]{3,4,2,1,0:T(8,128)S(1)}, f32[1,1,6,256,128]{3,4,2,1,0:T(8,128)}, u32[]{:S(2)}) copy-start(f32[1,1,6,256,128]{3,4,2,1,0:T(8,128)} %copy.254) | copy-start | bytes 2359300
  1560.4 17.8 %collective-permute-start.26 = (f32[256,128]{0,1:T(8,128)}, f32[256,128]{0,1:T(8,128)}, u32[]{:S(2)}, u32[]{:S(2)}) collective-permute-start(f32[256,128]{0,1:T(8,128)} %broadcast_select_fusion.1), channel_id=1, source_target_pairs={{0,1},{1,2},{2,3},{3,4},{4,5},{5,6},{6,7},{7,8},{8,9},{9,10},{10,1... | collective-permute-start | bytes 393224 | tf_op jit(solution)/shard_map/ppermute | solution.py:21
  1560.5 23.9 %collective-permute-start.28 = (f32[256,128]{0,1:T(8,128)}, f32[256,128]{0,1:T(8,128)}, u32[]{:S(2)}, u32[]{:S(2)}) collective-permute-start(f32[256,128]{0,1:T(8,128)} %broadcast_select_fusion), channel_id=1, source_target_pairs={{0,64},{64,128},{128,192},{192,0},{1,65},{65,129},{129,193},{193,1... | collective-permute-start | bytes 393224 | tf_op jit(solution)/shard_map/ppermute | solution.py:21
  1564.2 9.1 collective-permute-start.27
  1565.9 24.8 %collective-permute-start.29 = (f32[2,256,128]{1,2,0:T(8,128)}, f32[2,256,128]{1,2,0:T(8,128)}, u32[]{:S(2)}, u32[]{:S(2)}) collective-permute-start(f32[2,256,128]{1,2,0:T(8,128)} %pad_maximum_fusion.5), channel_id=1, source_target_pairs={{0,32},{1,33},{2,34},{3,35},{4,36},{5,37},{6,38},{7,39},{8,40},{9,... | collective-permute-start | bytes 786440 | tf_op jit(solution)/shard_map/ppermute | solution.py:31
  1568.3 109.8 %copy-start.17 = (f32[2,256,128]{1,2,0:T(8,128)S(1)}, f32[2,256,128]{1,2,0:T(8,128)}, u32[]{:S(2)}) copy-start(f32[2,256,128]{1,2,0:T(8,128)} %copy-done.16) | copy-start | bytes 786436
  (27 other events, 679.2 us)
Sparse Core Ops, SparseCore 0:
  10.9 2.5 sort.21.cloned.1.call-done
  (1 shorter events, 0.0 us)
where the time goes:
time: 1700 us; the launch traced here: 1690 us
  blocking collectives  1190 us (70%)
  starting transfers between devices  212 us (12%)
  local copies, waits for them, and re-layouts  131 us (8%)
  other arithmetic  76 us (4%)
  matrix products  45.8 us (3%)
  waiting for transfers between devices  20.2 us (1%)
    psum x3, blocking collectives, per_device(): gathered = lax.psum(selector[:, None, None] * projected[None], 'sub')  959 us
    psum x3, blocking collectives, per_device(): lax.psum((jnp.sum(residual * search, axis=(0, 1)), jnp.sum(search * assem...  231 us
    ppermute x12, starting transfers between devices, with_halo(): lax.ppermute(head, axis, [((i + 1) % count, i) for i in range(count)])  140 us
    ppermute x12, starting transfers between devices, with_halo(): lax.ppermute(tail, axis, [(i, (i + 1) % count) for i in range(count)])  70.9 us
    dot_general x3, matrix products, per_device(): jnp.dot(operator, local_copy.reshape(ORDER, COLS), precision=highest)  36.7 us
  transfers between devices with their start and end apart: 30, of which 6 were waited for; matrix products, arithmetic and copies ran while one was open for 5% of the time, Pallas kernels for 0%

commit v1 on v0

--- a/solution.py
+++ b/solution.py
@@ -95,9 +95,12 @@
             6, FACE, COLS
         )
         assembled = owned * (applied - partner_values(applied, pairing, inverse))
-        numerator, denominator = lax.psum(
-            (jnp.sum(residual * search, axis=(0, 1)), jnp.sum(search * assembled, axis=(0, 1))),
-            ("clus", "sub"),
+        numerator, denominator = jax.lax.psum(
+            jax.lax.psum(
+                (jnp.sum(residual * search, axis=(0, 1)), jnp.sum(search * assembled, axis=(0, 1))),
+                "sub",
+            ),
+            "clus",
         )
         step_size = damping_factor * numerator / denominator
         multipliers = multipliers + step_size * search

time: 1700 us -> 2060 us (1.21)
  blocking collectives: 1190 us -> 1560 us
    psum x3 -> x6, blocking collectives: 231 us -> 599 us  [the longest x3 497 us: per_device(): jax.lax.psum((jnp.sum(residual * search, axis=(0, 1)), jnp.sum(search * a...]
  transfers between devices with their start and end apart: 30 -> 30, of which waited for: 6 -> 5; matrix products, arithmetic and copies ran while one was open for 5% -> 4% of each run, Pallas kernels for 0% -> 0%
where the time goes in v1:
time: 2060 us
  blocking collectives  1560 us (76%)
  starting transfers between devices  205 us (10%)
  local copies, waits for them, and re-layouts  132 us (6%)
  other arithmetic  76.2 us (4%)
  matrix products  45.8 us (2%)
  waiting for transfers between devices  24.8 us (1%)
    psum x3, blocking collectives, per_device(): gathered = lax.psum(selector[:, None, None] * projected[None], 'sub')  957 us
    psum x3, blocking collectives, per_device(): jax.lax.psum((jnp.sum(residual * search, axis=(0, 1)), jnp.sum(search * a...  497 us
    ppermute x12, starting transfers between devices, with_halo(): lax.ppermute(head, axis, [((i + 1) % count, i) for i in range(count)])  138 us
    psum x3, blocking collectives, per_device(): jax.lax.psum(jax.lax.psum((jnp.sum(residual * search, axis=(0, 1)), jnp.s...  102 us
    ppermute x12, starting transfers between devices, with_halo(): lax.ppermute(tail, axis, [(i, (i + 1) % count) for i in range(count)])  65.9 us
  transfers between devices with their start and end apart: 30, of which 5 were waited for; matrix products, arithmetic and copies ran while one was open for 4% of the time, Pallas kernels for 0%

profile of v1, /device:TPU:1, one launch (start us, length us, event | category | flops | bytes accessed | tf_op | source)
XLA Modules:
  0.0 2056.1 jit_solution(11117957307006593966)
XLA Ops:
  22.3 326.6 %all-reduce.3 = (f32[2,32,128]{2,1,0:T(8,128)S(1)}, f32[2,32,32]{1,2,0:T(8,128)S(1)}) all-reduce(f32[2,32,128]{2,1,0:T(8,128)S(1)} %broadcast_multiply_fusion.3, f32[2,32,32]{1,2,0:T(8,128)S(1)} %broadcast_multiply_fusion.4), channel_id=1, replica_groups=mesh['clus'=4,'sub'=64] {'sub'}, use_global_device_ids=true, to_apply=%region_3.4 | all-reduce | flops 10240 | bytes 81920 | tf_op jit(solution)/shard_map/psum | solution.py:86
  349.0 5.9 custom-call.9
  355.1 4.9 custom-call.12
  360.5 1.8 convolution_bitcast_fusion.2
  363.7 2.1 multiply_subtract_fusion.9
  367.0 1.9 slice_bitcast_fusion.19
  373.3 56.8 %collective-permute-start.3 = (f32[256,128]{0,1:T(8,128)}, f32[256,128]{0,1:T(8,128)}, u32[]{:S(2)}, u32[]{:S(2)}) collective-permute-start(f32[256,128]{0,1:T(8,128)} %broadcast_select_fusion.10), channel_id=1, source_target_pairs={{0,64},{64,128},{128,192},{192,0},{1,65},{65,129},{129,193},{193,1... | collective-permute-start | bytes 393224 | tf_op jit(solution)/shard_map/ppermute | solution.py:21
  430.1 8.1 collective-permute-start
  439.5 3.8 collective-permute-done
  454.5 12.2 fusion.6
  472.0 8.7 collective-permute-start.5
  487.9 7.3 collective-permute-done.6
  497.9 1.6 multiply_reduce_fusion.5
  500.7 166.0 %all-reduce.2 = (f32[128]{0:T(128)S(1)}, f32[128]{0:T(128)S(1)}) all-reduce(f32[128]{0:T(128)S(1)} %get-tuple-element.13, f32[128]{0:T(128)S(1)} %get-tuple-element.12), channel_id=1, replica_groups=mesh['clus'=4,'sub'=64] {'sub'}, use_global_device_ids=true, to_apply=%region_9.12 | all-reduce | flops 256 | bytes 2048 | tf_op jit(solution)/shard_map/psum | solution.py:99
  666.7 33.7 %all-reduce.6 = (f32[128]{0:T(128)S(1)}, f32[128]{0:T(128)S(1)}) all-reduce(f32[128]{0:T(128)S(1)} %get-tuple-element.22, f32[128]{0:T(128)S(1)} %get-tuple-element.23), channel_id=1, replica_groups=mesh['clus'=4,'sub'=64] {'clus'}, use_global_device_ids=true, to_apply=%region_10.13 | all-reduce | flops 256 | bytes 2048 | tf_op jit(solution)/shard_map/psum | solution.py:98
  704.1 315.0 %psum.118 = f32[2,32,128]{2,1,0:T(8,128)S(1)} all-reduce(f32[2,32,128]{2,1,0:T(8,128)S(1)} %broadcast_multiply_fusion.2), channel_id=1, replica_groups=mesh['clus'=4,'sub'=64] {'sub'}, use_global_device_ids=true, to_apply=%region_11.14 | all-reduce | flops 8192 | bytes 65536 | tf_op jit(solution)/shard_map/psum | solution.py:86
  1021.5 2.3 copy.260
  1023.8 2.6 multiply_subtract_fusion.6
  1034.7 56.1 %collective-permute-start.12 = (f32[256,128]{0,1:T(8,128)}, f32[256,128]{0,1:T(8,128)S(1)}, u32[]{:S(2)}, u32[]{:S(2)}) collective-permute-start(f32[256,128]{0,1:T(8,128)} %get-tuple-element.59), channel_id=1, source_target_pairs={{64,0},{128,64},{192,128},{0,192},{65,1},{129,65},{193,129},{1,193... | collective-permute-start | bytes 393224 | tf_op jit(solution)/shard_map/ppermute | solution.py:23
  1092.1 2.3 copy.292
  1096.3 1.6 pad_maximum_fusion.2
  1101.6 4.5 collective-permute-done.11
  1115.5 12.1 fusion.9
  1133.0 1.6 collective-permute-start.17
  1134.6 4.4 collective-permute-start.15
  1143.0 1.6 pad_maximum_fusion.3
  1150.0 3.3 collective-permute-done.16
  1163.4 2.3 copy.294
  1165.7 1.9 multiply_reduce_fusion.3
  1167.5 165.9 %all-reduce.1 = (f32[128]{0:T(128)S(1)}, f32[128]{0:T(128)}) all-reduce(f32[128]{0:T(128)S(1)} %get-tuple-element.17, f32[128]{0:T(128)S(1)} %get-tuple-element.16), channel_id=1, replica_groups=mesh['clus'=4,'sub'=64] {'sub'}, use_global_device_ids=true, to_apply=%region_16.19 | all-reduce | flops 256 | bytes 2048 | tf_op jit(solution)/shard_map/psum | solution.py:99
  1333.4 33.9 %all-reduce.5 = (f32[128]{0:T(128)S(1)}, f32[128]{0:T(128)S(1)}) all-reduce(f32[128]{0:T(128)S(1)} %get-tuple-element.20, f32[128]{0:T(128)} %get-tuple-element.21), channel_id=1, replica_groups=mesh['clus'=4,'sub'=64] {'clus'}, use_global_device_ids=true, to_apply=%region_17.20 | all-reduce | flops 256 | bytes 2048 | tf_op jit(solution)/shard_map/psum | solution.py:98
  1371.6 315.2 %psum.123 = f32[2,32,128]{2,1,0:T(8,128)S(1)} all-reduce(f32[2,32,128]{2,1,0:T(8,128)S(1)} %broadcast_multiply_fusion.1), channel_id=1, replica_groups=mesh['clus'=4,'sub'=64] {'sub'}, use_global_device_ids=true, to_apply=%region_18.21 | all-reduce | flops 8192 | bytes 65536 | tf_op jit(solution)/shard_map/psum | solution.py:86
  1690.4 2.8 multiply_subtract_fusion.2
  1699.1 55.9 %collective-permute-start.22 = (f32[256,128]{0,1:T(8,128)}, f32[256,128]{0,1:T(8,128)S(1)}, u32[]{:S(2)}, u32[]{:S(2)}) collective-permute-start(f32[256,128]{0,1:T(8,128)} %get-tuple-element.47), channel_id=1, source_target_pairs={{64,0},{128,64},{192,128},{0,192},{65,1},{129,65},{193,129},{1,193... | collective-permute-start | bytes 393224 | tf_op jit(solution)/shard_map/ppermute | solution.py:23
  1756.3 2.3 copy.329
  1764.4 5.8 collective-permute-done.21
  1778.9 12.4 fusion.12
  1797.9 1.8 collective-permute-start.25
  1801.4 3.8 collective-permute-start.28
  1805.2 1.7 pad_maximum_fusion.5
  1811.3 1.8 bitcast_dynamic-update-slice_fusion.5
  1820.9 1.7 bitcast_dynamic-update-slice_fusion.3
  1822.6 1.6 bitcast_dynamic-update-slice_fusion.15
  1836.4 1.9 multiply_reduce_fusion.1
  1838.3 164.8 %all-reduce = (f32[128]{0:T(128)S(1)}, f32[128]{0:T(128)S(1)}) all-reduce(f32[128]{0:T(128)S(1)} %get-tuple-element.15, f32[128]{0:T(128)S(1)} %get-tuple-element.14), channel_id=1, replica_groups=mesh['clus'=4,'sub'=64] {'sub'}, use_global_device_ids=true, to_apply=%region_23.26 | all-reduce | flops 256 | bytes 2048 | tf_op jit(solution)/shard_map/psum | solution.py:99
  2003.1 34.2 %all-reduce.4 = (f32[128]{0:T(128)S(1)}, f32[128]{0:T(128)S(1)}) all-reduce(f32[128]{0:T(128)S(1)} %get-tuple-element.18, f32[128]{0:T(128)S(1)} %get-tuple-element.19), channel_id=1, replica_groups=mesh['clus'=4,'sub'=64] {'clus'}, use_global_device_ids=true, to_apply=%region_24.27 | all-reduce | flops 256 | bytes 2048 | tf_op jit(solution)/shard_map/psum | solution.py:98
  2037.3 1.7 bitcast_dynamic-update-slice_fusion.1
  2042.8 3.7 multiply_subtract_fusion
  (406 shorter events, 173.4 us)
Async XLA Ops:
  12.8 473.6 %copy-start.20 = (s32[1024]{0:T(1024)}, s32[1024]{0:T(1024)S(1)}, u32[]{:S(2)}) copy-start(s32[1024]{0:T(1024)S(1)} %pad_clamp_fusion.5) | copy-start | bytes 12292
  12.8 347.4 %copy-start.41 = (f32[2]{0:T(128)}, f32[2]{0:T(128)S(1)}, u32[]{:S(2)}) copy-start(f32[2]{0:T(128)S(1)} %compare_convert_fusion) | copy-start | bytes 28
  15.7 438.8 %copy-start.1 = (f32[1536,128]{0,1:T(8,128)}, f32[1536,128]{0,1:T(8,128)S(1)}, u32[]{:S(2)}) copy-start(f32[1536,128]{0,1:T(8,128)S(1)} %copy.224) | copy-start | bytes 2359300
  18.3 451.4 %copy-start.22 = (s32[1024]{0:T(1024)}, s32[1024]{0:T(1024)S(1)}, u32[]{:S(2)}) copy-start(s32[1024]{0:T(1024)S(1)} %pad_clamp_fusion.4) | copy-start | bytes 12292
  19.3 352.7 %copy-start.23 = (pred[256]{0:T(512)(128)(4,1)S(1)}, pred[256]{0:T(512)(128)(4,1)}, u32[]{:S(2)}) copy-start(pred[256]{0:T(512)(128)(4,1)} %get-tuple-element.93) | copy-start | bytes 772
  19.3 353.4 %copy-start.26 = (pred[256]{0:T(512)(128)(4,1)S(1)}, pred[256]{0:T(512)(128)(4,1)}, u32[]{:S(2)}) copy-start(pred[256]{0:T(512)(128)(4,1)} %get-tuple-element.92) | copy-start | bytes 772
  19.3 418.9 %copy-start.29 = (pred[256]{0:T(512)(128)(4,1)S(1)}, pred[256]{0:T(512)(128)(4,1)}, u32[]{:S(2)}) copy-start(pred[256]{0:T(512)(128)(4,1)} %get-tuple-element.91) | copy-start | bytes 772
  362.2 85.2 %copy-start.35 = (pred[256]{0:T(512)(128)(4,1)S(1)}, pred[256]{0:T(512)(128)(4,1)}, u32[]{:S(2)}) copy-start(pred[256]{0:T(512)(128)(4,1)} %compare_and_fusion.3) | copy-start | bytes 772
  363.7 86.9 %copy-start.32 = (pred[256]{0:T(512)(128)(4,1)S(1)}, pred[256]{0:T(512)(128)(4,1)}, u32[]{:S(2)}) copy-start(pred[256]{0:T(512)(128)(4,1)} %compare_and_fusion) | copy-start | bytes 772
  372.6 73.2 %collective-permute-start.1 = (f32[256,128]{0,1:T(8,128)}, f32[256,128]{0,1:T(8,128)}, u32[]{:S(2)}, u32[]{:S(2)}) collective-permute-start(f32[256,128]{0,1:T(8,128)} %broadcast_select_fusion.11), channel_id=1, source_target_pairs={{0,1},{1,2},{2,3},{3,4},{4,5},{5,6},{6,7},{7,8},{8,9},{9,10},{10,1... | collective-permute-start | bytes 393224 | tf_op jit(solution)/shard_map/ppermute | solution.py:21
  373.3 74.8 %collective-permute-start.3 = (f32[256,128]{0,1:T(8,128)}, f32[256,128]{0,1:T(8,128)}, u32[]{:S(2)}, u32[]{:S(2)}) collective-permute-start(f32[256,128]{0,1:T(8,128)} %broadcast_select_fusion.10), channel_id=1, source_target_pairs={{0,64},{64,128},{128,192},{192,0},{1,65},{65,129},{129,193},{193,1... | collective-permute-start | bytes 393224 | tf_op jit(solution)/shard_map/ppermute | solution.py:21
  430.1 8.4 collective-permute-start.2
  430.1 13.2 collective-permute-start
  438.2 11.4 collective-permute-start.4
  470.5 14.9 collective-permute-start.7
  472.0 14.3 collective-permute-start.5
  482.9 219.7 %copy-start = (f32[1,1,32,1536]{3,2,1,0:T(8,128)S(1)}, f32[1,1,32,1536]{3,2,1,0:T(8,128)}, u32[]{:S(2)}) copy-start(f32[1,1,32,1536]{3,2,1,0:T(8,128)} %param.11) | copy-start | bytes 589828
  484.0 11.3 collective-permute-start.6
  484.0 11.9 collective-permute-start.8
  485.4 10.6 collective-permute-start.9
  496.9 529.5 %copy-start.8 = (f32[256,128]{0,1:T(8,128)}, f32[256,128]{0,1:T(8,128)S(1)}, u32[]{:S(2)}) copy-start(f32[256,128]{0,1:T(8,128)S(1)} %copy.251) | copy-start | bytes 393220
  1023.8 86.8 %copy-start.33 = (pred[256]{0:T(512)(128)(4,1)S(1)}, pred[256]{0:T(512)(128)(4,1)}, u32[]{:S(2)}) copy-start(pred[256]{0:T(512)(128)(4,1)} %compare_and_fusion) | copy-start | bytes 772
  1027.6 87.9 %copy-start.4 = (f32[1536,128]{0,1:T(8,128)S(1)}, f32[1536,128]{0,1:T(8,128)}, u32[]{:S(2)}) copy-start(f32[1536,128]{0,1:T(8,128)} %copy-done.3) | copy-start | bytes 2359300
  1034.7 63.5 %collective-permute-start.12 = (f32[256,128]{0,1:T(8,128)}, f32[256,128]{0,1:T(8,128)S(1)}, u32[]{:S(2)}, u32[]{:S(2)}) collective-permute-start(f32[256,128]{0,1:T(8,128)} %get-tuple-element.59), channel_id=1, source_target_pairs={{64,0},{128,64},{192,128},{0,192},{65,1},{129,65},{193,129},{1,193... | collective-permute-start | bytes 393224 | tf_op jit(solution)/shard_map/ppermute | solution.py:23
  1090.8 8.3 collective-permute-start.10
  1094.4 11.6 collective-permute-start.11
  1095.9 11.1 collective-permute-start.13
  1098.0 10.0 collective-permute-start.14
  1133.0 11.7 collective-permute-start.17
  1134.6 11.9 collective-permute-start.15
  1142.2 11.1 collective-permute-start.16
  1142.2 12.6 collective-permute-start.18
  1144.6 11.1 collective-permute-start.19
  1160.7 532.5 %copy-start.13 = (f32[256,128]{0,1:T(8,128)}, f32[256,128]{0,1:T(8,128)S(1)}, u32[]{:S(2)}) copy-start(f32[256,128]{0,1:T(8,128)S(1)} %copy.287) | copy-start | bytes 393220
  1690.4 84.6 %copy-start.34 = (pred[256]{0:T(512)(128)(4,1)S(1)}, pred[256]{0:T(512)(128)(4,1)}, u32[]{:S(2)}) copy-start(pred[256]{0:T(512)(128)(4,1)} %compare_and_fusion) | copy-start | bytes 772
  1699.1 61.8 %collective-permute-start.22 = (f32[256,128]{0,1:T(8,128)}, f32[256,128]{0,1:T(8,128)S(1)}, u32[]{:S(2)}, u32[]{:S(2)}) collective-permute-start(f32[256,128]{0,1:T(8,128)} %get-tuple-element.47), channel_id=1, source_target_pairs={{64,0},{128,64},{192,128},{0,192},{65,1},{129,65},{193,129},{1,193... | collective-permute-start | bytes 393224 | tf_op jit(solution)/shard_map/ppermute | solution.py:23
  1755.0 6.8 collective-permute-start.20
  1758.6 11.6 collective-permute-start.21
  1760.1 12.4 collective-permute-start.23
  1760.5 13.6 collective-permute-start.24
  1797.9 239.4 %copy-start.9 = (f32[256,128]{0,1:T(8,128)S(1)}, f32[256,128]{0,1:T(8,128)}, u32[]{:S(2)}) copy-start(f32[256,128]{0,1:T(8,128)} %copy-done.8) | copy-start | bytes 393220
  1797.9 11.3 collective-permute-start.25
  1801.3 241.5 %copy-start.7 = (f32[1,1,6,256,128]{3,4,2,1,0:T(8,128)S(1)}, f32[1,1,6,256,128]{3,4,2,1,0:T(8,128)}, u32[]{:S(2)}) copy-start(f32[1,1,6,256,128]{3,4,2,1,0:T(8,128)} %copy.254) | copy-start | bytes 2359300
  1801.4 17.9 collective-permute-start.26
  1801.4 24.0 %collective-permute-start.28 = (f32[256,128]{0,1:T(8,128)}, f32[256,128]{0,1:T(8,128)}, u32[]{:S(2)}, u32[]{:S(2)}) collective-permute-start(f32[256,128]{0,1:T(8,128)} %broadcast_select_fusion), channel_id=1, source_target_pairs={{0,64},{64,128},{128,192},{192,0},{1,65},{65,129},{129,193},{193,1... | collective-permute-start | bytes 393224 | tf_op jit(solution)/shard_map/ppermute | solution.py:21
  1805.2 9.1 collective-permute-start.27
  1806.9 24.8 %collective-permute-start.29 = (f32[2,256,128]{1,2,0:T(8,128)}, f32[2,256,128]{1,2,0:T(8,128)}, u32[]{:S(2)}, u32[]{:S(2)}) collective-permute-start(f32[2,256,128]{1,2,0:T(8,128)} %pad_maximum_fusion.5), channel_id=1, source_target_pairs={{0,32},{1,33},{2,34},{3,35},{4,36},{5,37},{6,38},{7,39},{8,40},{9,... | collective-permute-start | bytes 786440 | tf_op jit(solution)/shard_map/ppermute | solution.py:31
  1809.2 232.9 %copy-start.17 = (f32[2,256,128]{1,2,0:T(8,128)S(1)}, f32[2,256,128]{1,2,0:T(8,128)}, u32[]{:S(2)}) copy-start(f32[2,256,128]{1,2,0:T(8,128)} %copy-done.16) | copy-start | bytes 786436
  (27 other events, 672.1 us)
Sparse Core Ops, SparseCore 0:
  10.9 2.5 sort.21.cloned.1.call-done
  (1 shorter events, 0.0 us)
